TPU v7x, 256 devices: a whole 4x4x8 slice. The times are simulated.
256 devices in a mesh: tile: 64 (over x, z_hi, y, core), lev: 4 (over z_lo).
Axes of the slice: x: 4, y: 4, z: 8 (z_hi: 2, z_lo: 4; z = z_hi * 4 + z_lo), core: 2. Of those that a mesh axis runs over, the one named last changes fastest.
Arguments:
- control: float32 [80, 32, 16384], P(None, 'lev', 'tile'), may hold values from -6 to 6
- ensemble: bfloat16 [80, 32, 16384], P(None, 'lev', 'tile'), may hold values from -6 to 6
- loc_blocks: bfloat16 [128, 9, 128, 128], P('tile'), may hold values from -0.1875 to 0.1875
- neighbours: int32 [128, 9], P('tile'), may hold values from 0 to 127, as said below
- vert_band: float32 [32, 9], replicated, may hold values from 0.1 to 0.6
- channel_weights: float32 [16, 32], P(None, 'lev'), may hold values from -1 to 1
- innovation: float32 [16, 16384], P(None, 'tile'), may hold values from -6 to 6
- inv_error: float32 [16, 16384], P(None, 'tile'), may hold values from 0.25 to 4
Outputs:
- grad_first: float32 [80, 32, 16384], P(None, 'lev', 'tile')
- grad_second: float32 [80, 32, 16384], P(None, 'lev', 'tile')
- costs: float32 [2], replicated
Inputs may be any that keep to these rules, and one draw needn't show every extreme that they name: neighbours[b,0] = b; neighbours[b,1] lies in tile b // 2 - 1 and neighbours[b,2] in tile b // 2 + 1, tiles counted cyclically modulo 64; every other entry lies in one of these three tiles; block n belongs to tile n // 2.
All inputs are finite; a program needn't handle non-finite values.
Results may differ from a plain program's by a relative error of at most 0.005.
Values may be sent and summed in bfloat16 or wider, within the bound.
No kernel may reach another device: no remote copies, remote signals or barrier semaphores. Data moves between devices by JAX's collectives and lax.ppermute only.
A program may use at most 64 MiB of HBM per device.

v0:
```python
import math
import jax
import jax.numpy as jnp
from jax import lax
from jax.sharding import PartitionSpec as P

HV = 4
step_length = 0.5


def with_halo(value, sides, width, wrap):
    for axis, dim in sides:
        peers, length = (lax.axis_size(axis), value.shape[dim])
        up = [(i, (i + 1) % peers) for i in range(peers if wrap else peers - 1)]
        down = [(j, i) for i, j in up]
        last = lax.slice_in_dim(value, length - width, length, axis=dim)
        first = lax.slice_in_dim(value, 0, width, axis=dim)
        before = lax.ppermute(last, axis, up)
        after = lax.ppermute(first, axis, down)
        value = jnp.concatenate([before, value, after], axis=dim)
    return value


def passed_along(value, axis, by):
    peers = lax.axis_size(axis)
    return lax.ppermute(value, axis, [(i, (i + by) % peers) for i in range(peers)])


def per_device(
    control, ensemble, loc_blocks, neighbours, vert_band, channel_weights, innovation, inv_error
):
    members, ldev, pdev = control.shape
    bpd = loc_blocks.shape[0]
    nbrs = loc_blocks.shape[1]
    ntile = lax.axis_size("tile")
    nlev = lax.axis_size("lev")
    tile_pos = lax.axis_index("tile")
    lev_pos = lax.axis_index("lev")
    norm_factor = 1.0 / math.sqrt(members - 1)
    offsets = jnp.mod(neighbours // bpd - tile_pos + 1, ntile)
    slots = (offsets * bpd + neighbours % bpd).reshape(-1)
    band_padded = jnp.pad(vert_band, ((HV, HV), (0, 0)))
    band_ext = lax.dynamic_slice_in_dim(band_padded, lev_pos * ldev, ldev + 2 * HV, 0)
    band_own = band_ext[HV : HV + ldev]
    ens_float = ensemble.astype(jnp.float32)

    def evaluate(field):
        extended = with_halo(field, (("lev", 1),), HV, False)
        smooth = jnp.zeros_like(field)
        for s in range(2 * HV + 1):
            smooth = smooth + band_own[:, s][None, :, None] * extended[:, s : s + ldev, :]
        smooth_half = smooth.astype(jnp.bfloat16)
        widened = with_halo(smooth_half, (("tile", 2),), pdev, True)
        picked = jnp.take(widened.reshape(members, ldev, 3 * bpd, 128), slots, axis=2)
        picked = picked.reshape(members, ldev, bpd, nbrs, 128)
        local_u = jnp.einsum(
            "mlbjc,bjic->mlbi", picked, loc_blocks, preferred_element_type=jnp.float32
        )
        local_u = local_u.reshape(members, ldev, pdev)
        incr = jnp.sum(ens_float * local_u, axis=0) * norm_factor
        partial_obs = jnp.einsum(
            "kl,lp->kp", channel_weights, incr, precision=lax.Precision.HIGHEST
        )
        evolved = lax.psum(partial_obs, "lev")
        misfit = evolved - innovation
        weighted = inv_error * misfit
        obs_term = jnp.where(lev_pos == 0, 0.5 * jnp.sum(weighted * misfit), 0.0)
        back_term = 0.5 * jnp.sum(field * field)
        incr_adj = jnp.einsum(
            "kl,kp->lp", channel_weights, weighted, precision=lax.Precision.HIGHEST
        )
        cotangent = (ens_float * incr_adj[None] * norm_factor).astype(jnp.bfloat16)
        terms = jnp.einsum(
            "mlbi,bjic->mlbjc",
            cotangent.reshape(members, ldev, bpd, 128),
            loc_blocks,
            preferred_element_type=jnp.float32,
        )
        spread = (
            jnp.zeros((members, ldev, 3 * bpd, 128), jnp.float32)
            .at[:, :, slots, :]
            .add(terms.reshape(members, ldev, bpd * nbrs, 128))
        )
        spread = spread.reshape(members, ldev, 3, pdev)
        adjoint = spread[:, :, 1] + passed_along(spread[:, :, 0], "tile", -1)
        adjoint = adjoint + passed_along(spread[:, :, 2], "tile", 1)
        adj_ext = with_halo(adjoint, (("lev", 1),), HV, False)
        gradient = field
        for s in range(2 * HV + 1):
            lower = 2 * HV - s
            gradient = (
                gradient
                + band_ext[lower : lower + ldev, s][None, :, None]
                * adj_ext[:, lower : lower + ldev, :]
            )
        return (gradient, back_term, obs_term)

    count = float(members * ldev * pdev * nlev * ntile)
    grad_first, back_first, obs_first = evaluate(control)
    back_first, obs_first, squares = lax.psum(
        (back_first, obs_first, jnp.sum(grad_first * grad_first)), ("tile", "lev")
    )
    tau = step_length / jnp.sqrt(squares / count + 1e-06)
    grad_second, back_second, obs_second = evaluate(control - tau * grad_first)
    back_second, obs_second = lax.psum((back_second, obs_second), ("tile", "lev"))
    costs = jnp.stack([back_first + obs_first, back_second + obs_second]) / count
    return (grad_first, grad_second, costs)


def solution(mesh):
    placed = (
        P(None, "lev", "tile"),
        P(None, "lev", "tile"),
        P("tile", None, None, None),
        P("tile", None),
        P(),
        P(None, "lev"),
        P(None, "tile"),
        P(None, "tile"),
    )
    return jax.shard_map(
        per_device,
        mesh=mesh,
        in_specs=placed,
        out_specs=(P(None, "lev", "tile"), P(None, "lev", "tile"), P()),
        check_vma=False,
    )
```

profile of v0, /device:TPU:1, one launch (start us, length us, event | category | flops | bytes accessed | tf_op | source)
XLA Modules:
  0.0 409.2 jit_solution(17185516404099371895)
XLA Ops:
  3.5 5.0 %collective-permute-start = (f32[80,4,256]{2,1,0:T(4,128)S(1)}, f32[80,4,256]{2,1,0:T(4,128)S(1)}, u32[]{:S(2)}, u32[]{:S(2)}) collective-permute-start(f32[80,4,256]{2,1,0:T(4,128)S(1)} %get-tuple-element.27), channel_id=1, source_target_pairs={{0,1},{1,2},{2,3},{4,5},{5,6},{6,7},{8,9},{9,10},{10,11},{12,13},{... | collective-permute-start | bytes 983048 | tf_op jit(solution)/shard_map/ppermute | solution.py:18
  19.3 3.3 collective-permute-done.2
  31.8 17.6 %psum.49 = f32[16,256]{1,0:T(8,128)S(1)} all-reduce(f32[16,256]{1,0:T(8,128)S(1)} %convolution_bitcast_fusion.5), channel_id=1, replica_groups=mesh['tile'=64,'lev'=4] {'lev'}, use_global_device_ids=true, to_apply=%region_1.3 | all-reduce | flops 4096 | bytes 32768 | tf_op jit(solution)/shard_map/psum | solution.py:64
  50.9 3.2 copy.35
  54.2 10.7 %scatter_fusion = f32[80,8,6,128]{3,1,2,0:T(8,128)S(1)} fusion(f32[80,8,6,128]{3,1,2,0:T(8,128)S(1)} %broadcast.72.clone, s32[18]{0:T(128)} %fusion.114, f32[18,80,8,128]{3,2,1,0:T(8,128)} %copy.35), kind=kCustom, calls=%fused_computation.2 | custom fusion | flops 1474560 | bytes 17694792 | tf_op jit(solution)/shard_map/scatter-add | solution.py:82
  66.9 4.4 %reshape.107 = f32[80,8,3,256]{3,2,1,0:T(4,128)} reshape(f32[80,8,6,128]{3,2,1,0:T(8,128)} %copy.36) | data formatting | bytes 3932160 | tf_op jit(solution)/shard_map/reshape | solution.py:84
  71.3 5.5 %fusion.119 = (f32[80,8,1,256]{3,2,1,0:T(1,128)S(1)}, f32[80,8,1,256]{3,2,1,0:T(1,128)S(1)}, f32[80,8,1,256]{3,2,1,0:T(1,128)S(1)}) fusion(f32[80,8,3,256]{3,2,1,0:T(4,128)} %reshape.107), kind=kLoop, calls=%fused_computation.235 | loop fusion | bytes 3932160 | tf_op jit(solution)/shard_map/slice | solution.py:85
  76.9 13.8 %collective-permute-start.4 = (f32[80,8,256]{2,1,0:T(8,128)S(1)}, f32[80,8,256]{2,1,0:T(8,128)S(1)}, u32[]{:S(2)}, u32[]{:S(2)}) collective-permute-start(f32[80,8,256]{2,1,0:T(8,128)S(1)} %bitcast.144), channel_id=1, source_target_pairs={{0,252},{4,0},{8,4},{12,8},{16,12},{20,16},{24,20},{28,24},{32,28}... | collective-permute-start | bytes 1966088 | tf_op jit(solution)/shard_map/ppermute | solution.py:26
  92.5 6.6 %collective-permute-done.5 = f32[80,8,256]{2,1,0:T(8,128)S(1)} collective-permute-done((f32[80,8,256]{2,1,0:T(8,128)S(1)}, f32[80,8,256]{2,1,0:T(8,128)S(1)}, u32[]{:S(2)}, u32[]{:S(2)}) %collective-permute-start.5) | collective-permute-done | bytes 655392 | tf_op jit(solution)/shard_map/ppermute | solution.py:26
  100.7 4.0 collective-permute-start.7
  105.5 8.9 %collective-permute-done.6 = f32[80,4,256]{2,1,0:T(4,128)S(1)} collective-permute-done((f32[80,4,256]{2,1,0:T(4,128)S(1)}, f32[80,4,256]{2,1,0:T(4,128)S(1)}, u32[]{:S(2)}, u32[]{:S(2)}) %collective-permute-start.6) | collective-permute-done | bytes 327712 | tf_op jit(solution)/shard_map/ppermute | solution.py:19
  117.1 91.2 %psum.50 = f32[]{:T(128)} all-reduce(f32[]{:T(128)} %get-tuple-element.10), channel_id=1, replica_groups=mesh['tile'=64,'lev'=4] {'tile','lev'}, use_global_device_ids=true, to_apply=%region_4.6 | all-reduce | flops 1 | bytes 8 | tf_op jit(solution)/shard_map/psum | solution.py:100
  213.7 4.9 %collective-permute-done.8 = f32[80,4,256]{2,1,0:T(4,128)S(1)} collective-permute-done((f32[80,4,256]{2,1,0:T(4,128)S(1)}, f32[80,4,256]{2,1,0:T(4,128)S(1)}, u32[]{:S(2)}, u32[]{:S(2)}) %collective-permute-start.8) | collective-permute-done | bytes 327712 | tf_op jit(solution)/shard_map/ppermute | solution.py:18
  218.6 3.9 collective-permute-done.9
  226.9 4.0 collective-permute-done.10
  240.1 12.1 %psum.51 = f32[16,256]{1,0:T(8,128)S(1)} all-reduce(f32[16,256]{1,0:T(8,128)S(1)} %convolution_bitcast_fusion.4), channel_id=1, replica_groups=mesh['tile'=64,'lev'=4] {'lev'}, use_global_device_ids=true, to_apply=%region_6.8 | all-reduce | flops 4096 | bytes 32768 | tf_op jit(solution)/shard_map/psum | solution.py:64
  253.7 3.2 copy.44
  257.0 10.5 %scatter_fusion.1 = f32[80,8,6,128]{3,1,2,0:T(8,128)S(1)} fusion(f32[80,8,6,128]{3,1,2,0:T(8,128)S(1)} %broadcast.72, s32[18]{0:T(128)S(1)} %copy-done.45, f32[18,80,8,128]{3,2,1,0:T(8,128)} %copy.44), kind=kCustom, calls=%fused_computation.3 | custom fusion | flops 1474560 | bytes 17694792 | tf_op jit(solution)/shard_map/scatter-add | solution.py:82
  269.6 4.4 %reshape.113 = f32[80,8,3,256]{3,2,1,0:T(4,128)} reshape(f32[80,8,6,128]{3,2,1,0:T(8,128)} %copy.45) | data formatting | bytes 3932160 | tf_op jit(solution)/shard_map/reshape | solution.py:84
  274.0 5.5 %fusion.118 = (f32[80,8,1,256]{3,2,1,0:T(1,128)S(1)}, f32[80,8,1,256]{3,2,1,0:T(1,128)S(1)}, f32[80,8,1,256]{3,2,1,0:T(1,128)S(1)}) fusion(f32[80,8,3,256]{3,2,1,0:T(4,128)} %reshape.113), kind=kLoop, calls=%fused_computation.234 | loop fusion | bytes 3932160 | tf_op jit(solution)/shard_map/slice | solution.py:85
  279.6 13.9 %collective-permute-start.12 = (f32[80,8,256]{2,1,0:T(8,128)S(1)}, f32[80,8,256]{2,1,0:T(8,128)S(1)}, u32[]{:S(2)}, u32[]{:S(2)}) collective-permute-start(f32[80,8,256]{2,1,0:T(8,128)S(1)} %bitcast.145), channel_id=1, source_target_pairs={{0,252},{4,0},{8,4},{12,8},{16,12},{20,16},{24,20},{28,24},{32,28}... | collective-permute-start | bytes 1966088 | tf_op jit(solution)/shard_map/ppermute | solution.py:26
  295.2 6.1 %collective-permute-done.13 = f32[80,8,256]{2,1,0:T(8,128)S(1)} collective-permute-done((f32[80,8,256]{2,1,0:T(8,128)S(1)}, f32[80,8,256]{2,1,0:T(8,128)S(1)}, u32[]{:S(2)}, u32[]{:S(2)}) %collective-permute-start.13) | collective-permute-done | bytes 655392 | tf_op jit(solution)/shard_map/ppermute | solution.py:26
  302.9 4.0 collective-permute-start.15
  310.0 95.2 %all-reduce.1 = (f32[]{:T(128)}, f32[]{:T(128)}) all-reduce(f32[]{:T(128)S(6)} %add.223, f32[]{:T(128)S(6)} %add.222), channel_id=1, replica_groups=mesh['tile'=64,'lev'=4] {'tile','lev'}, use_global_device_ids=true, to_apply=%region_13.15 | all-reduce | flops 2 | bytes 16 | tf_op jit(solution)/shard_map/psum | solution.py:105
  (169 shorter events, 62.7 us)
Async XLA Ops:
  2.2 11.7 %collective-permute-start.1 = (f32[80,4,256]{2,1,0:T(4,128)S(1)}, f32[80,4,256]{2,1,0:T(4,128)}, u32[]{:S(2)}, u32[]{:S(2)}) collective-permute-start(f32[80,4,256]{2,1,0:T(4,128)S(1)} %get-tuple-element.26), channel_id=1, source_target_pairs={{1,0},{2,1},{3,2},{5,4},{6,5},{7,6},{9,8},{10,9},{11,10},{13,12},{... | collective-permute-start | bytes 983048 | tf_op jit(solution)/shard_map/ppermute | solution.py:19
  3.5 11.4 %collective-permute-start = (f32[80,4,256]{2,1,0:T(4,128)S(1)}, f32[80,4,256]{2,1,0:T(4,128)S(1)}, u32[]{:S(2)}, u32[]{:S(2)}) collective-permute-start(f32[80,4,256]{2,1,0:T(4,128)S(1)} %get-tuple-element.27), channel_id=1, source_target_pairs={{0,1},{1,2},{2,3},{4,5},{5,6},{6,7},{8,9},{9,10},{10,11},{12,13},{... | collective-permute-start | bytes 983048 | tf_op jit(solution)/shard_map/ppermute | solution.py:18
  15.9 6.7 %collective-permute-start.2 = (bf16[80,8,256]{2,1,0:T(8,128)(2,1)S(1)}, bf16[80,8,256]{2,1,0:T(8,128)(2,1)S(1)}, u32[]{:S(2)}, u32[]{:S(2)}) collective-permute-start(bf16[80,8,256]{2,1,0:T(8,128)(2,1)S(1)} %fusion.78), channel_id=1, source_target_pairs={{0,4},{4,8},{8,12},{12,16},{16,20},{20,24},{24,28},{28,32},{32,36}... | collective-permute-start | bytes 983048 | tf_op jit(solution)/shard_map/ppermute | solution.py:18
  18.6 6.5 %collective-permute-start.3 = (bf16[80,8,256]{2,1,0:T(8,128)(2,1)S(1)}, bf16[80,8,256]{2,1,0:T(8,128)(2,1)S(1)}, u32[]{:S(2)}, u32[]{:S(2)}) collective-permute-start(bf16[80,8,256]{2,1,0:T(8,128)(2,1)S(1)} %fusion.78), channel_id=1, source_target_pairs={{4,0},{8,4},{12,8},{16,12},{20,16},{24,20},{28,24},{32,28},{36,32}... | collective-permute-start | bytes 983048 | tf_op jit(solution)/shard_map/ppermute | solution.py:19
  76.9 15.6 %collective-permute-start.4 = (f32[80,8,256]{2,1,0:T(8,128)S(1)}, f32[80,8,256]{2,1,0:T(8,128)S(1)}, u32[]{:S(2)}, u32[]{:S(2)}) collective-permute-start(f32[80,8,256]{2,1,0:T(8,128)S(1)} %bitcast.144), channel_id=1, source_target_pairs={{0,252},{4,0},{8,4},{12,8},{16,12},{20,16},{24,20},{28,24},{32,28}... | collective-permute-start | bytes 1966088 | tf_op jit(solution)/shard_map/ppermute | solution.py:26
  90.8 8.3 %collective-permute-start.5 = (f32[80,8,256]{2,1,0:T(8,128)S(1)}, f32[80,8,256]{2,1,0:T(8,128)S(1)}, u32[]{:S(2)}, u32[]{:S(2)}) collective-permute-start(f32[80,8,256]{2,1,0:T(8,128)S(1)} %bitcast.146), channel_id=1, source_target_pairs={{0,4},{4,8},{8,12},{12,16},{16,20},{20,24},{24,28},{28,32},{32,36}... | collective-permute-start | bytes 1966088 | tf_op jit(solution)/shard_map/ppermute | solution.py:26
  99.4 15.0 %collective-permute-start.6 = (f32[80,4,256]{2,1,0:T(4,128)S(1)}, f32[80,4,256]{2,1,0:T(4,128)S(1)}, u32[]{:S(2)}, u32[]{:S(2)}) collective-permute-start(f32[80,4,256]{2,1,0:T(4,128)S(1)} %get-tuple-element.24), channel_id=1, source_target_pairs={{1,0},{2,1},{3,2},{5,4},{6,5},{7,6},{9,8},{10,9},{11,10},{13,12},{... | collective-permute-start | bytes 983048 | tf_op jit(solution)/shard_map/ppermute | solution.py:19
  100.7 13.7 %collective-permute-start.7 = (f32[80,4,256]{2,1,0:T(4,128)S(1)}, f32[80,4,256]{2,1,0:T(4,128)S(1)}, u32[]{:S(2)}, u32[]{:S(2)}) collective-permute-start(f32[80,4,256]{2,1,0:T(4,128)S(1)} %get-tuple-element.25), channel_id=1, source_target_pairs={{0,1},{1,2},{2,3},{4,5},{5,6},{6,7},{8,9},{9,10},{10,11},{12,13},{... | collective-permute-start | bytes 983048 | tf_op jit(solution)/shard_map/ppermute | solution.py:18
  117.0 116.4 %copy-start.3 = (f32[80,8,256]{2,1,0:T(8,128)}, f32[80,8,256]{2,1,0:T(8,128)S(1)}, u32[]{:S(2)}) copy-start(f32[80,8,256]{2,1,0:T(8,128)S(1)} %get-tuple-element.11) | copy-start | bytes 1966084
  209.8 8.8 %collective-permute-start.8 = (f32[80,4,256]{2,1,0:T(4,128)S(1)}, f32[80,4,256]{2,1,0:T(4,128)S(1)}, u32[]{:S(2)}, u32[]{:S(2)}) collective-permute-start(f32[80,4,256]{2,1,0:T(4,128)S(1)} %get-tuple-element.22), channel_id=1, source_target_pairs={{0,1},{1,2},{2,3},{4,5},{5,6},{6,7},{8,9},{9,10},{10,11},{12,13},{... | collective-permute-start | bytes 983048 | tf_op jit(solution)/shard_map/ppermute | solution.py:18
  212.2 10.3 %collective-permute-start.9 = (f32[80,4,256]{2,1,0:T(4,128)S(1)}, f32[80,4,256]{2,1,0:T(4,128)S(1)}, u32[]{:S(2)}, u32[]{:S(2)}) collective-permute-start(f32[80,4,256]{2,1,0:T(4,128)S(1)} %get-tuple-element.23), channel_id=1, source_target_pairs={{1,0},{2,1},{3,2},{5,4},{6,5},{7,6},{9,8},{10,9},{11,10},{13,12},{... | collective-permute-start | bytes 983048 | tf_op jit(solution)/shard_map/ppermute | solution.py:19
  223.8 7.1 %collective-permute-start.10 = (bf16[80,8,256]{2,1,0:T(8,128)(2,1)S(1)}, bf16[80,8,256]{2,1,0:T(8,128)(2,1)S(1)}, u32[]{:S(2)}, u32[]{:S(2)}) collective-permute-start(bf16[80,8,256]{2,1,0:T(8,128)(2,1)S(1)} %fusion.31), channel_id=1, source_target_pairs={{0,4},{4,8},{8,12},{12,16},{16,20},{20,24},{24,28},{28,32},{32,36}... | collective-permute-start | bytes 983048 | tf_op jit(solution)/shard_map/ppermute | solution.py:18
  226.8 6.5 %collective-permute-start.11 = (bf16[80,8,256]{2,1,0:T(8,128)(2,1)S(1)}, bf16[80,8,256]{2,1,0:T(8,128)(2,1)S(1)}, u32[]{:S(2)}, u32[]{:S(2)}) collective-permute-start(bf16[80,8,256]{2,1,0:T(8,128)(2,1)S(1)} %fusion.31), channel_id=1, source_target_pairs={{4,0},{8,4},{12,8},{16,12},{20,16},{24,20},{28,24},{32,28},{36,32}... | collective-permute-start | bytes 983048 | tf_op jit(solution)/shard_map/ppermute | solution.py:19
  279.6 15.6 %collective-permute-start.12 = (f32[80,8,256]{2,1,0:T(8,128)S(1)}, f32[80,8,256]{2,1,0:T(8,128)S(1)}, u32[]{:S(2)}, u32[]{:S(2)}) collective-permute-start(f32[80,8,256]{2,1,0:T(8,128)S(1)} %bitcast.145), channel_id=1, source_target_pairs={{0,252},{4,0},{8,4},{12,8},{16,12},{20,16},{24,20},{28,24},{32,28}... | collective-permute-start | bytes 1966088 | tf_op jit(solution)/shard_map/ppermute | solution.py:26
  293.5 113.6 %copy-start.35 = (f32[8]{0:T(128)S(1)}, f32[8]{0:T(128)}, u32[]{:S(2)}) copy-start(f32[8]{0:T(128)} %get-tuple-element.28) | copy-start | bytes 100
  293.5 113.6 %copy-start.36 = (f32[8]{0:T(128)S(1)}, f32[8]{0:T(128)}, u32[]{:S(2)}) copy-start(f32[8]{0:T(128)} %get-tuple-element.37) | copy-start | bytes 100
  293.5 113.6 %copy-start.37 = (f32[8]{0:T(128)S(1)}, f32[8]{0:T(128)}, u32[]{:S(2)}) copy-start(f32[8]{0:T(128)} %get-tuple-element.39) | copy-start | bytes 100
  293.5 113.6 %copy-start.38 = (f32[8]{0:T(128)S(1)}, f32[8]{0:T(128)}, u32[]{:S(2)}) copy-start(f32[8]{0:T(128)} %get-tuple-element.40) | copy-start | bytes 100
  293.5 113.6 %copy-start.39 = (f32[8]{0:T(128)S(1)}, f32[8]{0:T(128)}, u32[]{:S(2)}) copy-start(f32[8]{0:T(128)} %get-tuple-element.41) | copy-start | bytes 100
  293.5 113.6 %copy-start.40 = (f32[8]{0:T(128)S(1)}, f32[8]{0:T(128)}, u32[]{:S(2)}) copy-start(f32[8]{0:T(128)} %get-tuple-element.42) | copy-start | bytes 100
  293.5 113.6 %copy-start.42 = (f32[8]{0:T(128)S(1)}, f32[8]{0:T(128)}, u32[]{:S(2)}) copy-start(f32[8]{0:T(128)} %copy-done.41) | copy-start | bytes 100
  293.6 7.7 %collective-permute-start.13 = (f32[80,8,256]{2,1,0:T(8,128)S(1)}, f32[80,8,256]{2,1,0:T(8,128)S(1)}, u32[]{:S(2)}, u32[]{:S(2)}) collective-permute-start(f32[80,8,256]{2,1,0:T(8,128)S(1)} %bitcast.147), channel_id=1, source_target_pairs={{0,4},{4,8},{8,12},{12,16},{16,20},{20,24},{24,28},{28,32},{32,36}... | collective-permute-start | bytes 1966088 | tf_op jit(solution)/shard_map/ppermute | solution.py:26
  301.6 105.5 %collective-permute-start.14 = (f32[80,4,256]{2,1,0:T(4,128)S(1)}, f32[80,4,256]{2,1,0:T(4,128)S(1)}, u32[]{:S(2)}, u32[]{:S(2)}) collective-permute-start(f32[80,4,256]{2,1,0:T(4,128)S(1)} %get-tuple-element.20), channel_id=1, source_target_pairs={{1,0},{2,1},{3,2},{5,4},{6,5},{7,6},{9,8},{10,9},{11,10},{13,12},{... | collective-permute-start | bytes 983048 | tf_op jit(solution)/shard_map/ppermute | solution.py:19
  302.9 104.2 %collective-permute-start.15 = (f32[80,4,256]{2,1,0:T(4,128)S(1)}, f32[80,4,256]{2,1,0:T(4,128)S(1)}, u32[]{:S(2)}, u32[]{:S(2)}) collective-permute-start(f32[80,4,256]{2,1,0:T(4,128)S(1)} %get-tuple-element.21), channel_id=1, source_target_pairs={{0,1},{1,2},{2,3},{4,5},{5,6},{6,7},{8,9},{9,10},{10,11},{12,13},{... | collective-permute-start | bytes 983048 | tf_op jit(solution)/shard_map/ppermute | solution.py:18
  (41 other events, 1520.8 us)
where the time goes:
time: 410 us; the launch traced here: 409 us
  blocking collectives  216 us (53%)
  starting transfers between devices  54.7 us (13%)
  waiting for transfers between devices  45.7 us (11%)
  local copies, waits for them, and re-layouts  43.7 us (11%)
  other arithmetic  40.1 us (10%)
  between operations  4.66 us (1%)
  matrix products  4.35 us (1%)
    psum x1, blocking collectives, per_device(): lax.psum((back_second, obs_second), ('tile', 'lev'))  95.2 us
    psum x1, blocking collectives, per_device(): lax.psum((back_first, obs_first, jnp.sum(grad_first * grad_first)), ('til...  91.2 us
    psum x2, blocking collectives, evaluate(): evolved = lax.psum(partial_obs, 'lev')  29.7 us
    ppermute x4, starting transfers between devices, passed_along(): lax.ppermute(value, axis, [(i, (i + by) % peers) for i in range(peers)])  27.9 us
    scatter-add x2, other arithmetic, evaluate(): spread = jnp.zeros((members, ldev, 3 * bpd, 128), jnp.float32).at[:, :, s...  21.2 us
    ppermute x6, starting transfers between devices, with_halo(): before = lax.ppermute(last, axis, up)  21.2 us
    ppermute x6, waiting for transfers between devices, with_halo(): after = lax.ppermute(first, axis, down)  17.7 us
    ppermute x4, waiting for transfers between devices, passed_along(): lax.ppermute(value, axis, [(i, (i + by) % peers) for i in range(peers)])  15.8 us
  transfers between devices with their start and end apart: 16, of which 11 were waited for; matrix products, arithmetic and copies ran while one was open for 2% of the time, Pallas kernels for 0%

commit v1 on v0

--- a/solution.py
+++ b/solution.py
@@ -98,7 +98,7 @@
     count = float(members * ldev * pdev * nlev * ntile)
     grad_first, back_first, obs_first = evaluate(control)
     back_first, obs_first, squares = lax.psum(
-        (back_first, obs_first, jnp.sum(grad_first * grad_first)), ("tile", "lev")
+        lax.psum((back_first, obs_first, jnp.sum(grad_first * grad_first)), "lev"), "tile"
     )
     tau = step_length / jnp.sqrt(squares / count + 1e-06)
     grad_second, back_second, obs_second = evaluate(control - tau * grad_first)

time: 410 us -> 763 us (1.86)
  blocking collectives: 216 us -> 568 us
    psum x1 -> x4, blocking collectives: 91.2 us -> 443 us  [the longest x2 423 us: per_device(): lax.psum(lax.psum((back_first, obs_first, jnp.sum(grad_first * grad_first...]
  transfers between devices with their start and end apart: 16 -> 16, of which waited for: 11 -> 11; matrix products, arithmetic and copies ran while one was open for 2% -> 1% of each run, Pallas kernels for 0% -> 0%
where the time goes in v1:
time: 763 us; the launch traced here: 760 us
  blocking collectives  568 us (74%)
  starting transfers between devices  54.4 us (7%)
  waiting for transfers between devices  44.2 us (6%)
  local copies, waits for them, and re-layouts  44.1 us (6%)
  other arithmetic  40.1 us (5%)
    psum x2, blocking collectives, per_device(): lax.psum(lax.psum((back_first, obs_first, jnp.sum(grad_first * grad_first...  423 us
    psum x1, blocking collectives, per_device(): lax.psum((back_second, obs_second), ('tile', 'lev'))  94.2 us
    psum x2, blocking collectives, evaluate(): evolved = lax.psum(partial_obs, 'lev')  30.4 us
    ppermute x4, starting transfers between devices, passed_along(): lax.ppermute(value, axis, [(i, (i + by) % peers) for i in range(peers)])  29.6 us
    scatter-add x2, other arithmetic, evaluate(): spread = jnp.zeros((members, ldev, 3 * bpd, 128), jnp.float32).at[:, :, s...  21.2 us
    psum x2, blocking collectives, per_device(): lax.psum((back_first, obs_first, jnp.sum(grad_first * grad_first)), 'lev')  19.9 us
    ppermute x6, waiting for transfers between devices, with_halo(): after = lax.ppermute(first, axis, down)  17.8 us
    ppermute x6, starting transfers between devices, with_halo(): before = lax.ppermute(last, axis, up)  17.2 us
  transfers between devices with their start and end apart: 16, of which 11 were waited for; matrix products, arithmetic and copies ran while one was open for 1% of the time, Pallas kernels for 0%

profile of v1, /device:TPU:1, one launch (start us, length us, event | category | flops | bytes accessed | tf_op | source)
XLA Modules:
  0.0 759.8 jit_solution(3573359180219789177)
XLA Ops:
  3.5 5.0 collective-permute-start
  19.3 3.3 collective-permute-done.2
  31.8 17.6 %psum.70 = f32[16,256]{1,0:T(8,128)S(1)} all-reduce(f32[16,256]{1,0:T(8,128)S(1)} %convolution_bitcast_fusion.5), channel_id=1, replica_groups=mesh['tile'=64,'lev'=4] {'lev'}, use_global_device_ids=true, to_apply=%region_1.3 | all-reduce | flops 4096 | bytes 32768 | tf_op jit(solution)/shard_map/psum | solution.py:64
  54.2 10.7 %scatter_fusion = f32[80,8,6,128]{3,1,2,0:T(8,128)S(1)} fusion(f32[80,8,6,128]{3,1,2,0:T(8,128)S(1)} %broadcast.72.clone, s32[18]{0:T(128)} %fusion.114, f32[18,80,8,128]{3,2,1,0:T(8,128)} %copy.35), kind=kCustom, calls=%fused_computation.2 | custom fusion | flops 1474560 | bytes 17694792 | tf_op jit(solution)/shard_map/scatter-add | solution.py:82
  67.0 4.4 reshape.107
  71.4 5.7 fusion.119
  77.1 13.9 %collective-permute-start.4 = (f32[80,8,256]{2,1,0:T(8,128)S(1)}, f32[80,8,256]{2,1,0:T(8,128)S(1)}, u32[]{:S(2)}, u32[]{:S(2)}) collective-permute-start(f32[80,8,256]{2,1,0:T(8,128)S(1)} %bitcast.144), channel_id=1, source_target_pairs={{0,252},{4,0},{8,4},{12,8},{16,12},{20,16},{24,20},{28,24},{32,28}... | collective-permute-start | bytes 1966088 | tf_op jit(solution)/shard_map/ppermute | solution.py:26
  92.7 6.7 collective-permute-done.5
  100.9 4.0 collective-permute-start.7
  105.7 8.9 %collective-permute-done.6 = f32[80,4,256]{2,1,0:T(4,128)S(1)} collective-permute-done((f32[80,4,256]{2,1,0:T(4,128)S(1)}, f32[80,4,256]{2,1,0:T(4,128)S(1)}, u32[]{:S(2)}, u32[]{:S(2)}) %collective-permute-start.6) | collective-permute-done | bytes 327712 | tf_op jit(solution)/shard_map/ppermute | solution.py:19
  117.3 10.0 %psum.71 = f32[]{:T(128)} all-reduce(f32[]{:T(128)} %get-tuple-element.8), channel_id=1, replica_groups=mesh['tile'=64,'lev'=4] {'lev'}, use_global_device_ids=true, to_apply=%region_4.6 | all-reduce | flops 1 | bytes 8 | tf_op jit(solution)/shard_map/psum | solution.py:101
  127.2 221.9 %psum.72 = f32[]{:T(128)} all-reduce(f32[]{:T(128)} %psum.71), channel_id=1, replica_groups=mesh['tile'=64,'lev'=4] {'tile'}, use_global_device_ids=true, to_apply=%region_5.7 | all-reduce | flops 1 | bytes 8 | tf_op jit(solution)/shard_map/psum | solution.py:100
  353.7 4.8 collective-permute-done.8
  358.5 3.9 collective-permute-done.9
  377.0 12.8 %psum.73 = f32[16,256]{1,0:T(8,128)S(1)} all-reduce(f32[16,256]{1,0:T(8,128)S(1)} %convolution_bitcast_fusion.4), channel_id=1, replica_groups=mesh['tile'=64,'lev'=4] {'lev'}, use_global_device_ids=true, to_apply=%region_7.9 | all-reduce | flops 4096 | bytes 32768 | tf_op jit(solution)/shard_map/psum | solution.py:64
  394.7 10.5 %scatter_fusion.1 = f32[80,8,6,128]{3,1,2,0:T(8,128)S(1)} fusion(f32[80,8,6,128]{3,1,2,0:T(8,128)S(1)} %broadcast.72, s32[18]{0:T(128)S(1)} %copy-done.45, f32[18,80,8,128]{3,2,1,0:T(8,128)} %copy.44), kind=kCustom, calls=%fused_computation.3 | custom fusion | flops 1474560 | bytes 17694792 | tf_op jit(solution)/shard_map/scatter-add | solution.py:82
  407.3 4.4 reshape.113
  411.7 5.7 fusion.118
  417.5 15.6 %collective-permute-start.12 = (f32[80,8,256]{2,1,0:T(8,128)S(1)}, f32[80,8,256]{2,1,0:T(8,128)S(1)}, u32[]{:S(2)}, u32[]{:S(2)}) collective-permute-start(f32[80,8,256]{2,1,0:T(8,128)S(1)} %bitcast.145), channel_id=1, source_target_pairs={{0,252},{4,0},{8,4},{12,8},{16,12},{20,16},{24,20},{28,24},{32,28}... | collective-permute-start | bytes 1966088 | tf_op jit(solution)/shard_map/ppermute | solution.py:26
  434.8 6.5 collective-permute-done.13
  442.9 4.0 collective-permute-start.15
  450.1 9.9 %psum.82 = f32[]{:T(128)} all-reduce(f32[]{:T(128)S(6)} %add.228), channel_id=1, replica_groups=mesh['tile'=64,'lev'=4] {'lev'}, use_global_device_ids=true, to_apply=%region_10.12 | all-reduce | flops 1 | bytes 8 | tf_op jit(solution)/shard_map/psum | solution.py:101
  460.0 94.2 %psum.81 = f32[]{:T(128)} all-reduce(f32[]{:T(128)S(6)} %add.229), channel_id=1, replica_groups=mesh['tile'=64,'lev'=4] {'tile','lev'}, use_global_device_ids=true, to_apply=%region_16.18 | all-reduce | flops 1 | bytes 8 | tf_op jit(solution)/shard_map/psum | solution.py:105
  554.2 201.5 %psum.80 = f32[]{:T(128)} all-reduce(f32[]{:T(128)} %psum.82), channel_id=1, replica_groups=mesh['tile'=64,'lev'=4] {'tile'}, use_global_device_ids=true, to_apply=%region_11.13 | all-reduce | flops 1 | bytes 8 | tf_op jit(solution)/shard_map/psum | solution.py:100
  (172 shorter events, 69.2 us)
Async XLA Ops:
  2.2 11.6 %collective-permute-start.1 = (f32[80,4,256]{2,1,0:T(4,128)S(1)}, f32[80,4,256]{2,1,0:T(4,128)}, u32[]{:S(2)}, u32[]{:S(2)}) collective-permute-start(f32[80,4,256]{2,1,0:T(4,128)S(1)} %get-tuple-element.24), channel_id=1, source_target_pairs={{1,0},{2,1},{3,2},{5,4},{6,5},{7,6},{9,8},{10,9},{11,10},{13,12},{... | collective-permute-start | bytes 983048 | tf_op jit(solution)/shard_map/ppermute | solution.py:19
  3.5 11.4 %collective-permute-start = (f32[80,4,256]{2,1,0:T(4,128)S(1)}, f32[80,4,256]{2,1,0:T(4,128)S(1)}, u32[]{:S(2)}, u32[]{:S(2)}) collective-permute-start(f32[80,4,256]{2,1,0:T(4,128)S(1)} %get-tuple-element.25), channel_id=1, source_target_pairs={{0,1},{1,2},{2,3},{4,5},{5,6},{6,7},{8,9},{9,10},{10,11},{12,13},{... | collective-permute-start | bytes 983048 | tf_op jit(solution)/shard_map/ppermute | solution.py:18
  15.8 6.8 collective-permute-start.2
  18.6 6.5 collective-permute-start.3
  77.1 15.6 %collective-permute-start.4 = (f32[80,8,256]{2,1,0:T(8,128)S(1)}, f32[80,8,256]{2,1,0:T(8,128)S(1)}, u32[]{:S(2)}, u32[]{:S(2)}) collective-permute-start(f32[80,8,256]{2,1,0:T(8,128)S(1)} %bitcast.144), channel_id=1, source_target_pairs={{0,252},{4,0},{8,4},{12,8},{16,12},{20,16},{24,20},{28,24},{32,28}... | collective-permute-start | bytes 1966088 | tf_op jit(solution)/shard_map/ppermute | solution.py:26
  91.0 8.3 %collective-permute-start.5 = (f32[80,8,256]{2,1,0:T(8,128)S(1)}, f32[80,8,256]{2,1,0:T(8,128)S(1)}, u32[]{:S(2)}, u32[]{:S(2)}) collective-permute-start(f32[80,8,256]{2,1,0:T(8,128)S(1)} %bitcast.146), channel_id=1, source_target_pairs={{0,4},{4,8},{8,12},{12,16},{16,20},{20,24},{24,28},{28,32},{32,36}... | collective-permute-start | bytes 1966088 | tf_op jit(solution)/shard_map/ppermute | solution.py:26
  99.6 15.0 %collective-permute-start.6 = (f32[80,4,256]{2,1,0:T(4,128)S(1)}, f32[80,4,256]{2,1,0:T(4,128)S(1)}, u32[]{:S(2)}, u32[]{:S(2)}) collective-permute-start(f32[80,4,256]{2,1,0:T(4,128)S(1)} %get-tuple-element.22), channel_id=1, source_target_pairs={{1,0},{2,1},{3,2},{5,4},{6,5},{7,6},{9,8},{10,9},{11,10},{13,12},{... | collective-permute-start | bytes 983048 | tf_op jit(solution)/shard_map/ppermute | solution.py:19
  100.9 13.7 %collective-permute-start.7 = (f32[80,4,256]{2,1,0:T(4,128)S(1)}, f32[80,4,256]{2,1,0:T(4,128)S(1)}, u32[]{:S(2)}, u32[]{:S(2)}) collective-permute-start(f32[80,4,256]{2,1,0:T(4,128)S(1)} %get-tuple-element.23), channel_id=1, source_target_pairs={{0,1},{1,2},{2,3},{4,5},{5,6},{6,7},{8,9},{9,10},{10,11},{12,13},{... | collective-permute-start | bytes 983048 | tf_op jit(solution)/shard_map/ppermute | solution.py:18
  350.8 7.6 %collective-permute-start.8 = (f32[80,4,256]{2,1,0:T(4,128)S(1)}, f32[80,4,256]{2,1,0:T(4,128)S(1)}, u32[]{:S(2)}, u32[]{:S(2)}) collective-permute-start(f32[80,4,256]{2,1,0:T(4,128)S(1)} %get-tuple-element.20), channel_id=1, source_target_pairs={{0,1},{1,2},{2,3},{4,5},{5,6},{6,7},{8,9},{9,10},{10,11},{12,13},{... | collective-permute-start | bytes 983048 | tf_op jit(solution)/shard_map/ppermute | solution.py:18
  352.2 10.1 %collective-permute-start.9 = (f32[80,4,256]{2,1,0:T(4,128)S(1)}, f32[80,4,256]{2,1,0:T(4,128)S(1)}, u32[]{:S(2)}, u32[]{:S(2)}) collective-permute-start(f32[80,4,256]{2,1,0:T(4,128)S(1)} %get-tuple-element.21), channel_id=1, source_target_pairs={{1,0},{2,1},{3,2},{5,4},{6,5},{7,6},{9,8},{10,9},{11,10},{13,12},{... | collective-permute-start | bytes 983048 | tf_op jit(solution)/shard_map/ppermute | solution.py:19
  363.6 4.1 collective-permute-start.10
  363.7 6.6 collective-permute-start.11
  417.5 17.3 %collective-permute-start.12 = (f32[80,8,256]{2,1,0:T(8,128)S(1)}, f32[80,8,256]{2,1,0:T(8,128)S(1)}, u32[]{:S(2)}, u32[]{:S(2)}) collective-permute-start(f32[80,8,256]{2,1,0:T(8,128)S(1)} %bitcast.145), channel_id=1, source_target_pairs={{0,252},{4,0},{8,4},{12,8},{16,12},{20,16},{24,20},{28,24},{32,28}... | collective-permute-start | bytes 1966088 | tf_op jit(solution)/shard_map/ppermute | solution.py:26
  433.1 324.5 %copy-start.35 = (f32[8]{0:T(128)S(1)}, f32[8]{0:T(128)}, u32[]{:S(2)}) copy-start(f32[8]{0:T(128)} %get-tuple-element.26) | copy-start | bytes 100
  433.1 324.5 %copy-start.36 = (f32[8]{0:T(128)S(1)}, f32[8]{0:T(128)}, u32[]{:S(2)}) copy-start(f32[8]{0:T(128)} %get-tuple-element.35) | copy-start | bytes 100
  433.1 324.5 %copy-start.37 = (f32[8]{0:T(128)S(1)}, f32[8]{0:T(128)}, u32[]{:S(2)}) copy-start(f32[8]{0:T(128)} %get-tuple-element.37) | copy-start | bytes 100
  433.1 324.5 %copy-start.38 = (f32[8]{0:T(128)S(1)}, f32[8]{0:T(128)}, u32[]{:S(2)}) copy-start(f32[8]{0:T(128)} %get-tuple-element.38) | copy-start | bytes 100
  433.1 324.5 %copy-start.39 = (f32[8]{0:T(128)S(1)}, f32[8]{0:T(128)}, u32[]{:S(2)}) copy-start(f32[8]{0:T(128)} %get-tuple-element.39) | copy-start | bytes 100
  433.1 324.5 %copy-start.40 = (f32[8]{0:T(128)S(1)}, f32[8]{0:T(128)}, u32[]{:S(2)}) copy-start(f32[8]{0:T(128)} %get-tuple-element.40) | copy-start | bytes 100
  433.2 324.5 %copy-start.42 = (f32[8]{0:T(128)S(1)}, f32[8]{0:T(128)}, u32[]{:S(2)}) copy-start(f32[8]{0:T(128)} %copy-done.41) | copy-start | bytes 100
  433.2 324.5 %copy-start.44 = (f32[8]{0:T(128)S(1)}, f32[8]{0:T(128)}, u32[]{:S(2)}) copy-start(f32[8]{0:T(128)} %copy-done.43) | copy-start | bytes 100
  433.2 8.1 %collective-permute-start.13 = (f32[80,8,256]{2,1,0:T(8,128)S(1)}, f32[80,8,256]{2,1,0:T(8,128)S(1)}, u32[]{:S(2)}, u32[]{:S(2)}) collective-permute-start(f32[80,8,256]{2,1,0:T(8,128)S(1)} %bitcast.147), channel_id=1, source_target_pairs={{0,4},{4,8},{8,12},{12,16},{16,20},{20,24},{24,28},{28,32},{32,36}... | collective-permute-start | bytes 1966088 | tf_op jit(solution)/shard_map/ppermute | solution.py:26
  441.6 316.0 %collective-permute-start.14 = (f32[80,4,256]{2,1,0:T(4,128)S(1)}, f32[80,4,256]{2,1,0:T(4,128)S(1)}, u32[]{:S(2)}, u32[]{:S(2)}) collective-permute-start(f32[80,4,256]{2,1,0:T(4,128)S(1)} %get-tuple-element.18), channel_id=1, source_target_pairs={{1,0},{2,1},{3,2},{5,4},{6,5},{7,6},{9,8},{10,9},{11,10},{13,12},{... | collective-permute-start | bytes 983048 | tf_op jit(solution)/shard_map/ppermute | solution.py:19
  442.9 314.7 %collective-permute-start.15 = (f32[80,4,256]{2,1,0:T(4,128)S(1)}, f32[80,4,256]{2,1,0:T(4,128)S(1)}, u32[]{:S(2)}, u32[]{:S(2)}) collective-permute-start(f32[80,4,256]{2,1,0:T(4,128)S(1)} %get-tuple-element.19), channel_id=1, source_target_pairs={{0,1},{1,2},{2,3},{4,5},{5,6},{6,7},{8,9},{9,10},{10,11},{12,13},{... | collective-permute-start | bytes 983048 | tf_op jit(solution)/shard_map/ppermute | solution.py:18
  (41 other events, 3131.7 us)
